TPU v7x, 32 devices: a whole 2x2x4 slice. The times are simulated.
32 devices in a mesh: ctx: 8 (over z, x), head: 4 (over y, core).
Axes of the slice: x: 2, y: 2, z: 4, core: 2. Of those that a mesh axis runs over, the one named last changes fastest.
Arguments:
- attn_query: bfloat16 [4096, 6144], P('ctx', 'head'), may hold values from -16 to 16
- attn_key: bfloat16 [4096, 6144], P('ctx', 'head'), may hold values from -16 to 16
- attn_value: bfloat16 [4096, 6144], P('ctx', 'head'), may hold values from -120 to 120
- delta_query: bfloat16 [4096, 6144], P('ctx', 'head'), may hold values from -6 to 6
- delta_key: bfloat16 [4096, 6144], P('ctx', 'head'), may hold values from -6 to 6
- delta_value: bfloat16 [4096, 6144], P('ctx', 'head'), may hold values from -120 to 120
- delta_gate: float32 [4096, 48], P('ctx', 'head'), may hold values from 0.5 to 1
- delta_beta: float32 [4096, 48], P('ctx', 'head'), may hold values from 0 to 0.6, as said below
- attn_gain: float32 [6144], P('head'), may hold values from 0.1 to 1.9
- delta_gain: float32 [6144], P('head'), may hold values from 0.1 to 1.9
Outputs:
- mixed: bfloat16 [4096, 6144], P('ctx', 'head')
Inputs may be any that keep to these rules, and one draw needn't show every extreme that they name: `delta_beta`: Positive.
All inputs are finite; a program needn't handle non-finite values.
Results may differ from a plain program's by a relative error of at most 0.004.
Values may be sent and summed in bfloat16 or wider, within the bound.
A program may use at most 192 MiB of HBM per device.

v0:
```python
import functools
import math

import jax
import jax.numpy as jnp
from jax import lax
from jax.experimental import pallas as pl
from jax.experimental.pallas import tpu as pltpu
from jax.sharding import PartitionSpec as P

DH = 128
WINDOW = 1024
CHUNK = 128
QROWS = 256
HALO_AHEAD = 12
RELAY_LAG = 3
HEADS_STEP = 2

epsilon = 1e-06
f32 = jnp.float32
bf16 = jnp.bfloat16


def dot(left, right, dims=((1,), (0,))):
    return lax.dot_general(left, right, (dims, ((), ())), preferred_element_type=f32)


def dot1(left, right, dims=((1,), (0,))):
    return dot(left.astype(bf16), right.astype(bf16), dims)


def split(value):
    high = value.astype(bf16)
    return high, (value - high.astype(f32)).astype(bf16)


def dot3(left, right, dims=((1,), (0,))):
    lh, ll = split(left)
    rh, rl = split(right)
    return dot(lh, rh, dims) + (dot(lh, rl, dims) + dot(ll, rh, dims))


def unit_scale(raw):
    wide = raw.astype(f32)
    mean = jnp.mean(wide * wide, axis=-1, keepdims=True)
    return lax.rsqrt(mean + epsilon) / math.sqrt(DH)


def delta_heads(first, q_ref, k_ref, v_ref, gate_ref, beta_ref, out_ref, qeff_ref, lin_ref, off_ref):
    rows = q_ref.shape[0]
    chunks = rows // CHUNK
    ri = lax.broadcasted_iota(jnp.int32, (CHUNK, CHUNK), 0)
    ci = lax.broadcasted_iota(jnp.int32, (CHUNK, CHUNK), 1)
    eye = ri == ci
    lower = ri >= ci
    strict = ri > ci
    identity = jnp.where(eye, 1.0, 0.0).astype(f32)

    def column(row):
        return jnp.sum(jnp.where(eye, row, 0.0), axis=1, keepdims=True)

    def as_row(col):
        return jnp.sum(jnp.where(eye, col, 0.0), axis=0, keepdims=True)

    units = [(h, c) for c in range(chunks) for h in range(HEADS_STEP)]
    terms = {}
    for h, c in units:
        rs = slice(c * CHUNK, (c + 1) * CHUNK)
        cs = pl.ds(pl.multiple_of((first + h) * DH, DH), DH)
        q, k = q_ref[rs, cs], k_ref[rs, cs]
        log_row = jnp.log(gate_ref[first + h, :, rs])
        log_col = column(log_row)
        beta_col = column(beta_ref[first + h, :, rs])
        sum_row = jnp.sum(jnp.where(ri <= ci, log_col, 0.0), axis=0, keepdims=True)
        sum_col = jnp.sum(jnp.where(lower, log_row, 0.0), axis=1, keepdims=True)
        total = jnp.sum(log_row, axis=1, keepdims=True)
        sk, sq = unit_scale(k), unit_scale(q)
        sk_row = as_row(sk)
        ratios = jnp.exp(jnp.where(lower, sum_col - sum_row, -1e30)) * sk_row
        both = dot(jnp.concatenate([k, q], axis=0), k, ((1,), (1,)))
        low = jnp.where(strict, (beta_col * sk) * ratios * both[:CHUNK], 0.0)
        mix = (sq * ratios) * both[CHUNK:]
        growth = jnp.exp(sum_col)
        terms[h, c] = dict(
            low=low,
            mix=mix.astype(bf16),
            inv=identity - jnp.where((ri // 2) == (ci // 2), low, 0.0),
            beta=beta_col,
            gk=growth * sk,
            gq=growth * sq,
            tail=jnp.exp(total - sum_col) * sk,
            last=jnp.exp(total),
        )
    size = 2
    while size < CHUNK:
        pick = ((ri // (2 * size)) == (ci // (2 * size))) & ((ri // size) != (ci // size))
        for u in units:
            t = terms[u]
            t["tmp"] = dot1(jnp.where(pick, t["low"], 0.0), t["inv"])
        for u in units:
            t = terms[u]
            t["inv"] = t["inv"] - dot1(t["inv"], t["tmp"])
        size *= 2
    states = [None] * HEADS_STEP
    for c in range(chunks):
        rs = slice(c * CHUNK, (c + 1) * CHUNK)
        for h in range(HEADS_STEP):
            cs = pl.ds(pl.multiple_of((first + h) * DH, DH), DH)
            t = terms[h, c]
            q, k, v = q_ref[rs, cs], k_ref[rs, cs], v_ref[rs, cs].astype(f32)
            zero = jnp.zeros((CHUNK, DH), f32)
            if c == 0:
                state = jnp.concatenate([jnp.zeros((DH, DH), f32), identity], axis=1)
                ks = jnp.concatenate([zero, k.astype(f32)], axis=1)
                qs = jnp.concatenate([zero, q.astype(f32)], axis=1)
            else:
                state = states[h]
                sb = state.astype(bf16)
                kqs = dot(jnp.concatenate([k, q], axis=0), sb)
                ks, qs = kqs[:CHUNK], kqs[CHUNK:]
            resid = jnp.concatenate([v, zero], axis=1) - t["gk"] * ks
            errors = dot1(t["inv"], t["beta"] * resid)
            out = t["gq"] * qs + dot(t["mix"], errors.astype(bf16))
            out_ref[first + h, rs] = out[:, :DH]
            qeff_ref[first + h, rs] = out[:, DH:].astype(bf16)
            states[h] = t["last"] * state + dot(
                k, (t["tail"] * errors).astype(bf16), ((0,), (0,))
            )
    for h in range(HEADS_STEP):
        off_ref[first + h] = states[h][:, :DH]
        lin_ref[first + h] = states[h][:, DH:]


def layer_kernel(
    aq_ref, ak_ref, av_ref, dq_ref, dk_ref, dv_ref, gate_ref, beta_ref, again_ref, dgain_ref,
    mixed_ref,
    keys, vals, attn_out, delta_out, qeff, linear, offset, entering, leaving, attn_sq, delta_sq,
    sums_send, sums_recv,
    own_sem, far_send, far_recv, near_send, near_recv, relay_send, relay_recv, sums_ss, sums_rs,
    *, contexts, groups,
):
    rows, width = aq_ref.shape
    heads = width // DH
    me = lax.axis_index("ctx")
    group = lax.axis_index("head")
    odd = lax.rem(me, 2) == 1
    even = lax.rem(me, 2) == 0
    back = WINDOW
    halves = rows // QROWS
    blocks = rows // CHUNK

    barrier = pltpu.get_barrier_semaphore()
    for by in (-2, -1, 1, 2):
        @pl.when((me + by >= 0) & (me + by < contexts))
        def _():
            pl.semaphore_signal(
                barrier, inc=1, device_id={"ctx": me + by}, device_id_type=pl.DeviceIdType.MESH
            )
    for by in range(1, groups):
        pl.semaphore_signal(
            barrier, inc=1, device_id={"head": lax.rem(group + by, groups)},
            device_id_type=pl.DeviceIdType.MESH,
        )
    near_peers = jnp.minimum(me, 2) + jnp.minimum(contexts - 1 - me, 2)
    pl.semaphore_wait(barrier, near_peers + (groups - 1))

    both = ((0, ak_ref, keys), (1, av_ref, vals))
    far_rows = pl.ds(0, rows)
    near_rows = pl.ds(rows, rows)
    own_rows = pl.ds(back, rows)

    def lanes(h):
        return pl.ds(pl.multiple_of(h * DH, DH), DH)

    def own_copy(h, kind, source, buffer):
        return pltpu.make_async_copy(
            source.at[:, lanes(h)], buffer.at[h, own_rows], own_sem.at[kind, h]
        )

    def far_copy(h, kind, source, buffer):
        return pltpu.make_async_remote_copy(
            src_ref=source.at[:, lanes(h)],
            dst_ref=buffer.at[h, far_rows],
            send_sem=far_send.at[kind, h],
            recv_sem=far_recv.at[kind, h],
            device_id={"ctx": lax.rem(me + 2, contexts)},
            device_id_type=pl.DeviceIdType.MESH,
        )

    def near_copy(h, kind, source, buffer):
        return pltpu.make_async_remote_copy(
            src_ref=source.at[:, lanes(h)],
            dst_ref=buffer.at[h, near_rows],
            send_sem=near_send.at[kind, h],
            recv_sem=near_recv.at[kind, h],
            device_id={"ctx": lax.rem(me + 1, contexts)},
            device_id_type=pl.DeviceIdType.MESH,
        )

    def forward_copy(h, kind, source, buffer):
        return pltpu.make_async_remote_copy(
            src_ref=buffer.at[h, far_rows],
            dst_ref=buffer.at[h, near_rows],
            send_sem=near_send.at[kind, h],
            recv_sem=near_recv.at[kind, h],
            device_id={"ctx": lax.rem(me + contexts - 1, contexts)},
            device_id_type=pl.DeviceIdType.MESH,
        )

    def relay_copy(h):
        return pltpu.make_async_remote_copy(
            src_ref=leaving.at[h],
            dst_ref=entering.at[h],
            send_sem=relay_send.at[h],
            recv_sem=relay_recv.at[h],
            device_id={"ctx": lax.rem(me + 1, contexts)},
            device_id_type=pl.DeviceIdType.MESH,
        )

    def send_halo(h):
        @pl.when(h < heads)
        def _():
            @pl.when(me + 2 < contexts)
            def _():
                for args in both:
                    far_copy(h, *args).start()

            @pl.when(even)
            def _():
                for args in both:
                    near_copy(h, *args).start()

    def forward(h):
        @pl.when(odd & (me >= 3))
        def _():
            for args in both:
                far_copy(h, *args).wait_recv()
                forward_copy(h, *args).start()

    def start_own(h, carry):
        for args in both:
            own_copy(h, *args).start()
        return carry

    lax.fori_loop(0, min(HALO_AHEAD, heads), lambda h, c: (send_halo(h), c)[1], 0)
    lax.fori_loop(0, heads, start_own, 0)

    @pl.when(me < 2)
    def _():
        def clear(h, carry):
            keys[h, far_rows] = jnp.zeros((rows, DH), bf16)
            vals[h, far_rows] = jnp.zeros((rows, DH), bf16)
            return carry
        lax.fori_loop(0, heads, clear, 0)

    @pl.when(me < 1)
    def _():
        def clear(h, carry):
            keys[h, near_rows] = jnp.zeros((rows, DH), bf16)
            vals[h, near_rows] = jnp.zeros((rows, DH), bf16)
            entering[h] = jnp.zeros((DH, DH), f32)
            return carry
        lax.fori_loop(0, heads, clear, 0)

    attn_sq[...] = jnp.zeros_like(attn_sq)
    delta_sq[...] = jnp.zeros_like(delta_sq)
    steps = heads // HEADS_STEP

    def delta_step(i, carry):
        delta_heads(
            i * HEADS_STEP, dq_ref, dk_ref, dv_ref, gate_ref, beta_ref,
            delta_out, qeff, linear, offset,
        )

        @pl.when(i >= 1)
        def _():
            forward(i - 1)

        send_halo(HALO_AHEAD + i)
        return carry

    lax.fori_loop(0, steps, delta_step, 0)

    scale = math.log2(math.e) / math.sqrt(DH)
    ri = lax.broadcasted_iota(jnp.int32, (QROWS, QROWS), 0)
    ci = lax.broadcasted_iota(jnp.int32, (QROWS, QROWS), 1)
    tiles = WINDOW // QROWS + 1
    first_tile = jnp.maximum(WINDOW - me * rows, 0) // QROWS

    def attend(h, b):
        q_rows = pl.ds(pl.multiple_of(b * QROWS, QROWS), QROWS)
        q = aq_ref[q_rows, lanes(h)]
        scores = []
        for n in range(tiles):
            at = pl.ds(pl.multiple_of((b + n) * QROWS, QROWS), QROWS)
            s = dot(q, keys[h, at], ((1,), (1,))) * scale
            if n < tiles - 1:
                s = s + jnp.where(b + n >= first_tile, 0.0, -1e30).astype(f32)
            if n == 0:
                s = jnp.where(ci > ri, s, -1e30)
            if n == tiles - 1:
                s = jnp.where(ci <= ri, s, -1e30)
            scores.append(s)
        top = jnp.max(functools.reduce(jnp.maximum, scores), axis=1, keepdims=True)
        raised = [jnp.exp2(s - top) for s in scores]
        total = jnp.sum(functools.reduce(jnp.add, raised), axis=1, keepdims=True)
        inverse = 1.0 / total
        out = None
        for n in range(tiles):
            at = pl.ds(pl.multiple_of((b + n) * QROWS, QROWS), QROWS)
            part = dot((raised[n] * inverse).astype(bf16), vals[h, at])
            out = part if out is None else out + part
        attn_out[h, q_rows] = out
        attn_sq[q_rows, :] += out * out

    def relay(h):
        @pl.when(me >= 1)
        def _():
            relay_copy(h).wait_recv()

        state = entering[h]

        @pl.when(me + 1 < contexts)
        def _():
            leaving[h] = dot3(linear[h], state) + offset[h]
            relay_copy(h).start()

        high, low = split(state)
        q = qeff[h]
        full = delta_out[h] + (dot(q, high) + dot(q, low))
        delta_out[h] = full
        delta_sq[...] += full * full

    def step(j, carry):
        h, b = j // halves, lax.rem(j, halves)

        @pl.when(h < heads)
        def _():
            @pl.when(b == 0)
            def _():
                @pl.when(h >= steps - 1)
                def _():
                    forward(h)

                for args in both:
                    own_copy(h, *args).wait()

                    @pl.when((me >= 2) & jnp.logical_not(odd & (me >= 3)))
                    def _():
                        far_copy(h, *args).wait_recv()

                    @pl.when(me >= 1)
                    def _():
                        near_copy(h, *args).wait_recv()

                send_halo(h + HALO_AHEAD + steps)

            attend(h, b)

        r = j - RELAY_LAG * me

        @pl.when((r >= 0) & (r < heads))
        def _():
            relay(r)

        return carry

    turns = max(heads * halves, RELAY_LAG * (contexts - 1) + heads)
    lax.fori_loop(0, turns, step, 0)

    dr = lax.broadcasted_iota(jnp.int32, (CHUNK, CHUNK), 0)
    dc = lax.broadcasted_iota(jnp.int32, (CHUNK, CHUNK), 1)
    eye = dr == dc
    lines = []
    for part in (attn_sq, delta_sq):
        for b in range(blocks):
            col = jnp.sum(part[b * CHUNK : (b + 1) * CHUNK, :], axis=1, keepdims=True)
            lines.append(jnp.sum(jnp.where(eye, col, 0.0), axis=0, keepdims=True))
    mine = jnp.concatenate(lines, axis=0)
    sums_send[...] = mine

    def sums_copy(by):
        return pltpu.make_async_remote_copy(
            src_ref=sums_send,
            dst_ref=sums_recv.at[by],
            send_sem=sums_ss.at[by],
            recv_sem=sums_rs.at[by],
            device_id={"head": lax.rem(group + by, groups)},
            device_id_type=pl.DeviceIdType.MESH,
        )

    for by in range(1, groups):
        sums_copy(by).start()
    whole = mine
    for by in range(1, groups):
        sums_copy(by).wait_recv()
        whole = whole + sums_recv[by]
    scales = lax.rsqrt(whole / (width * groups) + epsilon) * 0.5
    for b in range(blocks):
        rs = slice(b * CHUNK, (b + 1) * CHUNK)
        sa = jnp.sum(jnp.where(eye, scales[b : b + 1], 0.0), axis=1, keepdims=True)
        sd = jnp.sum(
            jnp.where(eye, scales[blocks + b : blocks + b + 1], 0.0), axis=1, keepdims=True
        )
        for h in range(heads):
            cs = slice(h * DH, (h + 1) * DH)
            mixed_ref[rs, cs] = (
                again_ref[:, cs] * attn_out[h, rs] * sa + dgain_ref[:, cs] * delta_out[h, rs] * sd
            ).astype(bf16)

    for by in range(1, groups):
        sums_copy(by).wait_send()

    def drain(h, carry):
        for args in both:
            @pl.when(me + 2 < contexts)
            def _():
                far_copy(h, *args).wait_send()

            @pl.when(even)
            def _():
                near_copy(h, *args).wait_send()

            @pl.when(odd & (me >= 3))
            def _():
                forward_copy(h, *args).wait_send()

        @pl.when(me + 1 < contexts)
        def _():
            relay_copy(h).wait_send()

        return carry

    lax.fori_loop(0, heads, drain, 0)


def on_device(
    attn_query,
    attn_key,
    attn_value,
    delta_query,
    delta_key,
    delta_value,
    delta_gate,
    delta_beta,
    attn_gain,
    delta_gain,
):
    rows, width = attn_query.shape
    heads = width // DH
    groups = lax.axis_size("head")
    lines = 2 * rows // CHUNK
    vmem = pl.BlockSpec(memory_space=pltpu.VMEM)
    hbm = pl.BlockSpec(memory_space=pl.ANY)
    dma = pltpu.SemaphoreType.DMA
    return pl.pallas_call(
        functools.partial(layer_kernel, contexts=lax.axis_size("ctx"), groups=groups),
        in_specs=[vmem, hbm, hbm] + [vmem] * 7,
        out_specs=vmem,
        out_shape=jax.ShapeDtypeStruct((rows, width), bf16),
        scratch_shapes=[
            pltpu.VMEM((heads, WINDOW + rows, DH), bf16),
            pltpu.VMEM((heads, WINDOW + rows, DH), bf16),
            pltpu.VMEM((heads, rows, DH), f32),
            pltpu.VMEM((heads, rows, DH), f32),
            pltpu.VMEM((heads, rows, DH), bf16),
            pltpu.VMEM((heads, DH, DH), f32),
            pltpu.VMEM((heads, DH, DH), f32),
            pltpu.VMEM((heads, DH, DH), f32),
            pltpu.VMEM((heads, DH, DH), f32),
            pltpu.VMEM((rows, DH), f32),
            pltpu.VMEM((rows, DH), f32),
            pltpu.VMEM((lines, CHUNK), f32),
            pltpu.VMEM((groups, lines, CHUNK), f32),
            dma((2, heads)),
            dma((2, heads)),
            dma((2, heads)),
            dma((2, heads)),
            dma((2, heads)),
            dma((heads,)),
            dma((heads,)),
            dma((groups,)),
            dma((groups,)),
        ],
        compiler_params=pltpu.CompilerParams(
            collective_id=0, has_side_effects=True, vmem_limit_bytes=60 * 1024 * 1024
        ),
        name="layer",
    )(
        attn_query,
        attn_key,
        attn_value,
        delta_query,
        delta_key,
        delta_value,
        delta_gate.T[:, None, :],
        delta_beta.T[:, None, :],
        attn_gain[None, :],
        delta_gain[None, :],
    )


def solution(mesh):
    both = P("ctx", "head")
    return jax.shard_map(
        on_device,
        mesh=mesh,
        in_specs=(both,) * 8 + (P("head"),) * 2,
        out_specs=both,
        check_vma=False,
    )
```

profile of v0, /device:TPU:27, one launch (start us, length us, event | category | flops | bytes accessed | tf_op | source)
XLA Modules:
  0.0 157.5 jit_solution(7495807338513426609)
XLA Ops:
  0.0 1.3 broadcast_in_dim.14.again_ref
  1.3 1.3 broadcast_in_dim.15.dgain_ref
  2.6 1.4 broadcast_in_dim.12.gate_ref
  4.0 1.4 broadcast_in_dim.13.beta_ref
  5.3 149.5 %layer.1 = bf16[512,1536]{1,0:T(8,128)(2,1)} custom-call(bf16[512,1536]{1,0:T(8,128)(2,1)} %aq_ref.1, bf16[512,1536]{1,0:T(8,128)(2,1)} %ak_ref.1, bf16[512,1536]{1,0:T(8,128)(2,1)} %av_ref.1, bf16[512,1536]{1,0:T(8,128)(2,1)} %dq_ref.1, bf16[512,1536]{1,0:T(8,128)(2,1)} %dk_ref.1, bf16[512,1536]{1,0:T(8,128)(2,1)} %dv_ref.1, ...), custom_call_target="tpu_custom_call" | custom-call | tf_op jit(solution)/shard_map/layer/pallas_call | solution.py:456
  154.8 2.7 %copy.12 = bf16[512,1536]{1,0:T(8,128)(2,1)} copy(bf16[512,1536]{1,0:T(8,128)(2,1)} %layer.1) | data formatting | bytes 3145728
where the time goes:
time: 158 us; the launch traced here: 157 us
  Pallas kernels  149 us (94%)
  local copies, waits for them, and re-layouts  7.99 us (5%)
    pallas_call x1, Pallas kernels, on_device(): pl.pallas_call(functools.partial(layer_kernel, contexts=lax.axis_size('ct...  149 us

commit v1 on v0

--- a/solution.py
+++ b/solution.py
@@ -12,8 +12,8 @@
 WINDOW = 1024
 CHUNK = 128
 QROWS = 256
-HALO_AHEAD = 12
-RELAY_LAG = 3
+HALO_AHEAD = 1
+RELAY_LAG = 5
 HEADS_STEP = 2
 
 epsilon = 1e-06
@@ -132,11 +132,11 @@
 
 
 def layer_kernel(
-    aq_ref, ak_ref, av_ref, dq_ref, dk_ref, dv_ref, gate_ref, beta_ref, again_ref, dgain_ref,
-    mixed_ref,
+    aq_ref, ak_ref, av_ref, dq_ref, dk_ref, dv_ref, gates_ref, betas_ref, again_ref, dgain_ref,
+    mixed_hbm,
     keys, vals, attn_out, delta_out, qeff, linear, offset, entering, leaving, attn_sq, delta_sq,
-    sums_send, sums_recv,
-    own_sem, far_send, far_recv, near_send, near_recv, relay_send, relay_recv, sums_ss, sums_rs,
+    sums_send, sums_recv, gate_ref, beta_ref, mixed_ref,
+    out_sem, own_sem, far_send, far_recv, near_send, near_recv, relay_send, relay_recv, sums_ss, sums_rs,
     *, contexts, groups,
 ):
     rows, width = aq_ref.shape
@@ -149,21 +149,6 @@
     halves = rows // QROWS
     blocks = rows // CHUNK
 
-    barrier = pltpu.get_barrier_semaphore()
-    for by in (-2, -1, 1, 2):
-        @pl.when((me + by >= 0) & (me + by < contexts))
-        def _():
-            pl.semaphore_signal(
-                barrier, inc=1, device_id={"ctx": me + by}, device_id_type=pl.DeviceIdType.MESH
-            )
-    for by in range(1, groups):
-        pl.semaphore_signal(
-            barrier, inc=1, device_id={"head": lax.rem(group + by, groups)},
-            device_id_type=pl.DeviceIdType.MESH,
-        )
-    near_peers = jnp.minimum(me, 2) + jnp.minimum(contexts - 1 - me, 2)
-    pl.semaphore_wait(barrier, near_peers + (groups - 1))
-
     both = ((0, ak_ref, keys), (1, av_ref, vals))
     far_rows = pl.ds(0, rows)
     near_rows = pl.ds(rows, rows)
@@ -179,7 +164,7 @@
 
     def far_copy(h, kind, source, buffer):
         return pltpu.make_async_remote_copy(
-            src_ref=source.at[:, lanes(h)],
+            src_ref=buffer.at[h, own_rows],
             dst_ref=buffer.at[h, far_rows],
             send_sem=far_send.at[kind, h],
             recv_sem=far_recv.at[kind, h],
@@ -189,7 +174,7 @@
 
     def near_copy(h, kind, source, buffer):
         return pltpu.make_async_remote_copy(
-            src_ref=source.at[:, lanes(h)],
+            src_ref=buffer.at[h, own_rows],
             dst_ref=buffer.at[h, near_rows],
             send_sem=near_send.at[kind, h],
             recv_sem=near_recv.at[kind, h],
@@ -242,8 +227,30 @@
             own_copy(h, *args).start()
         return carry
 
+    lax.fori_loop(0, heads, start_own, 0)
+
+    barrier = pltpu.get_barrier_semaphore()
+    for by in (-2, -1, 1, 2):
+        @pl.when((me + by >= 0) & (me + by < contexts))
+        def _():
+            pl.semaphore_signal(
+                barrier, inc=1, device_id={"ctx": me + by}, device_id_type=pl.DeviceIdType.MESH
+            )
+    for by in range(1, groups):
+        pl.semaphore_signal(
+            barrier, inc=1, device_id={"head": lax.rem(group + by, groups)},
+            device_id_type=pl.DeviceIdType.MESH,
+        )
+    near_peers = jnp.minimum(me, 2) + jnp.minimum(contexts - 1 - me, 2)
+    pl.semaphore_wait(barrier, near_peers + (groups - 1))
+
+    def wait_own(h, carry):
+        for args in both:
+            own_copy(h, *args).wait()
+        return carry
+
+    lax.fori_loop(0, heads, wait_own, 0)
     lax.fori_loop(0, min(HALO_AHEAD, heads), lambda h, c: (send_halo(h), c)[1], 0)
-    lax.fori_loop(0, heads, start_own, 0)
 
     @pl.when(me < 2)
     def _():
@@ -262,6 +269,10 @@
             return carry
         lax.fori_loop(0, heads, clear, 0)
 
+    gate_rows, beta_rows = gates_ref[...].T, betas_ref[...].T
+    for h in range(heads):
+        gate_ref[h] = gate_rows[h : h + 1]
+        beta_ref[h] = beta_rows[h : h + 1]
     attn_sq[...] = jnp.zeros_like(attn_sq)
     delta_sq[...] = jnp.zeros_like(delta_sq)
     steps = heads // HEADS_STEP
@@ -343,8 +354,6 @@
                     forward(h)
 
                 for args in both:
-                    own_copy(h, *args).wait()
-
                     @pl.when((me >= 2) & jnp.logical_not(odd & (me >= 3)))
                     def _():
                         far_copy(h, *args).wait_recv()
@@ -396,6 +405,11 @@
         sums_copy(by).wait_recv()
         whole = whole + sums_recv[by]
     scales = lax.rsqrt(whole / (width * groups) + epsilon) * 0.5
+
+    def out_copy(b):
+        span = pl.ds(b * CHUNK, CHUNK)
+        return pltpu.make_async_copy(mixed_ref.at[span], mixed_hbm.at[span], out_sem.at[b])
+
     for b in range(blocks):
         rs = slice(b * CHUNK, (b + 1) * CHUNK)
         sa = jnp.sum(jnp.where(eye, scales[b : b + 1], 0.0), axis=1, keepdims=True)
@@ -405,9 +419,12 @@
         for h in range(heads):
             cs = slice(h * DH, (h + 1) * DH)
             mixed_ref[rs, cs] = (
-                again_ref[:, cs] * attn_out[h, rs] * sa + dgain_ref[:, cs] * delta_out[h, rs] * sd
+                again_ref[cs][None, :] * attn_out[h, rs] * sa + dgain_ref[cs][None, :] * delta_out[h, rs] * sd
             ).astype(bf16)
-
+        out_copy(b).start()
+
+    for b in range(blocks):
+        out_copy(b).wait()
     for by in range(1, groups):
         sums_copy(by).wait_send()
 
@@ -456,7 +473,7 @@
     return pl.pallas_call(
         functools.partial(layer_kernel, contexts=lax.axis_size("ctx"), groups=groups),
         in_specs=[vmem, hbm, hbm] + [vmem] * 7,
-        out_specs=vmem,
+        out_specs=hbm,
         out_shape=jax.ShapeDtypeStruct((rows, width), bf16),
         scratch_shapes=[
             pltpu.VMEM((heads, WINDOW + rows, DH), bf16),
@@ -472,6 +489,10 @@
             pltpu.VMEM((rows, DH), f32),
             pltpu.VMEM((lines, CHUNK), f32),
             pltpu.VMEM((groups, lines, CHUNK), f32),
+            pltpu.VMEM((heads, 1, rows), f32),
+            pltpu.VMEM((heads, 1, rows), f32),
+            pltpu.VMEM((rows, width), bf16),
+            dma((rows // CHUNK,)),
             dma((2, heads)),
             dma((2, heads)),
             dma((2, heads)),
@@ -493,10 +514,10 @@
         delta_query,
         delta_key,
         delta_value,
-        delta_gate.T[:, None, :],
-        delta_beta.T[:, None, :],
-        attn_gain[None, :],
-        delta_gain[None, :],
+        delta_gate,
+        delta_beta,
+        attn_gain,
+        delta_gain,
     )
 
 

time: 158 us -> 140 us (0.89)
  Pallas kernels: 149 us -> 134 us
  local copies, waits for them, and re-layouts: 7.99 us -> 5.86 us
    pallas_call x1, Pallas kernels: 149 us -> 134 us  [on_device(): pl.pallas_call(functools.partial(layer_kernel, contexts=lax.axis_size('ct...]
    broadcast_in_dim x4 -> x0, local copies, waits for them, and re-layouts: 5.33 us -> none  [the longest x1 1.38 us: on_device(): delta_gate.T[:, None, :]]
    unnamed x1 -> x3, local copies, waits for them, and re-layouts: 2.65 us -> 5.86 us
where the time goes in v1:
time: 140 us
  Pallas kernels  134 us (96%)
  local copies, waits for them, and re-layouts  5.86 us (4%)
    pallas_call x1, Pallas kernels, on_device(): pl.pallas_call(functools.partial(layer_kernel, contexts=lax.axis_size('ct...  134 us
    unnamed x3, local copies, waits for them, and re-layouts  5.86 us

profile of v1, /device:TPU:27, one launch (start us, length us, event | category | flops | bytes accessed | tf_op | source)
XLA Modules:
  0.0 139.6 jit_solution(13965600152715602928)
XLA Ops:
  0.0 1.6 %copy.11.gates_ref = f32[512,12]{1,0:T(8,128)} copy(f32[512,12]{0,1:T(8,128)} %param.16) | data formatting | bytes 49152 | tf_op args[6]
  1.6 1.6 %copy.12.betas_ref = f32[512,12]{1,0:T(8,128)} copy(f32[512,12]{0,1:T(8,128)} %param.17) | data formatting | bytes 49152 | tf_op args[7]
  3.2 133.7 %layer.1 = bf16[512,1536]{1,0:T(8,128)(2,1)} custom-call(bf16[512,1536]{1,0:T(8,128)(2,1)} %aq_ref.1, bf16[512,1536]{1,0:T(8,128)(2,1)} %ak_ref.1, bf16[512,1536]{1,0:T(8,128)(2,1)} %av_ref.1, bf16[512,1536]{1,0:T(8,128)(2,1)} %dq_ref.1, bf16[512,1536]{1,0:T(8,128)(2,1)} %dk_ref.1, bf16[512,1536]{1,0:T(8,128)(2,1)} %dv_ref.1, f32[512,12]{1,0:T(8,128)} %copy.11.gates_ref, ...), custom_call_target="tpu_custom_call" | custom-call | tf_op jit(solution)/shard_map/layer/pallas_call | solution.py:473
  137.0 2.7 %copy.14 = bf16[512,1536]{1,0:T(8,128)(2,1)} copy(bf16[512,1536]{1,0:T(8,128)(2,1)} %layer.1) | data formatting | bytes 3145728

commit v2 on v1

--- a/solution.py
+++ b/solution.py
@@ -12,7 +12,7 @@
 WINDOW = 1024
 CHUNK = 128
 QROWS = 256
-HALO_AHEAD = 1
+HALO_AHEAD = 2
 RELAY_LAG = 5
 HEADS_STEP = 2
 

time: 140 us -> 140 us (level)
  no operation moved by 1% of the time
where the time goes in v2:
time: 140 us
  Pallas kernels  134 us (96%)
  local copies, waits for them, and re-layouts  5.86 us (4%)
    pallas_call x1, Pallas kernels, on_device(): pl.pallas_call(functools.partial(layer_kernel, contexts=lax.axis_size('ct...  134 us
    unnamed x3, local copies, waits for them, and re-layouts  5.86 us

profile of v2, /device:TPU:27, one launch (start us, length us, event | category | flops | bytes accessed | tf_op | source)
XLA Modules:
  0.0 140.0 jit_solution(8376237364873854359)
XLA Ops:
  0.0 1.6 %copy.11.gates_ref = f32[512,12]{1,0:T(8,128)} copy(f32[512,12]{0,1:T(8,128)} %param.16) | data formatting | bytes 49152 | tf_op args[6]
  1.6 1.6 %copy.12.betas_ref = f32[512,12]{1,0:T(8,128)} copy(f32[512,12]{0,1:T(8,128)} %param.17) | data formatting | bytes 49152 | tf_op args[7]
  3.2 134.2 %layer.1 = bf16[512,1536]{1,0:T(8,128)(2,1)} custom-call(bf16[512,1536]{1,0:T(8,128)(2,1)} %aq_ref.1, bf16[512,1536]{1,0:T(8,128)(2,1)} %ak_ref.1, bf16[512,1536]{1,0:T(8,128)(2,1)} %av_ref.1, bf16[512,1536]{1,0:T(8,128)(2,1)} %dq_ref.1, bf16[512,1536]{1,0:T(8,128)(2,1)} %dk_ref.1, bf16[512,1536]{1,0:T(8,128)(2,1)} %dv_ref.1, f32[512,12]{1,0:T(8,128)} %copy.11.gates_ref, ...), custom_call_target="tpu_custom_call" | custom-call | tf_op jit(solution)/shard_map/layer/pallas_call | solution.py:473
  137.4 2.7 %copy.14 = bf16[512,1536]{1,0:T(8,128)(2,1)} copy(bf16[512,1536]{1,0:T(8,128)(2,1)} %layer.1) | data formatting | bytes 3145728
